TPU v7x, 256 devices: a whole 4x4x8 slice. The times are simulated.
256 devices in a mesh: row: 16 (over y, z_hi, core), col: 16 (over z_lo, x).
Axes of the slice: x: 4, y: 4, z: 8 (z_hi: 2, z_lo: 4; z = z_hi * 4 + z_lo), core: 2. Of those that a mesh axis runs over, the one named last changes fastest.
Arguments:
- queries: bfloat16 [32, 16, 128, 2048], P('row', 'col'), may hold values from -70 to 70
- fine_keys: bfloat16 [32, 16, 128, 2048], P('row', 'col'), may hold values from -4 to 4
- fine_values: bfloat16 [32, 16, 128, 2048], P('row', 'col'), may hold values from -6 to 6
- keep_flags: int32 [32, 16, 9], P('row', 'col'), may hold values 0 or 1
- coarse_keys: bfloat16 [2048, 2048], P('col'), may hold values from -6 to 6
- coarse_values: bfloat16 [2048, 2048], P('col'), may hold values from -6 to 6
Outputs:
- attended: bfloat16 [32, 16, 128, 2048], P('row', 'col')
All inputs are finite; a program needn't handle non-finite values. No bound on the sum of `keep_flags` on one device may be relied on, other than what follows from the above.
Results may differ from a plain program's by a relative error of at most 0.0035.
Values may be sent and summed in bfloat16 or wider, within the bound.
A program may use at most 128 MiB of HBM per device.

v0:
```python
import jax
import jax.numpy as jnp
from jax import lax
from jax.sharding import PartitionSpec as P

HEADS = 16
HEAD_DIM = 128


def padded_2(cells, sides, width):
    for axis, dim in sides:
        count = lax.axis_size(axis)
        ends = count - 1
        head = lax.slice_in_dim(cells, 0, width, axis=dim)
        tail = lax.slice_in_dim(cells, cells.shape[dim] - width, cells.shape[dim], axis=dim)
        cells = jnp.concatenate(
            [
                lax.ppermute(tail, axis, [(i, (i + 1) % count) for i in range(ends)]),
                cells,
                lax.ppermute(head, axis, [((i + 1) % count, i) for i in range(ends)]),
            ],
            axis=dim,
        )
    return cells


def body(queries, fine_keys, fine_values, keep_flags, coarse_keys, coarse_values):
    rows_tiles, cols_tiles, tile_len, model_width = queries.shape
    tile_count = rows_tiles * cols_tiles
    scale = HEAD_DIM ** (-0.5)
    stacked = jnp.stack((fine_keys, fine_values), 0)
    padded = padded_2(stacked, (("row", 1), ("col", 2)), 1)
    far_keys, far_values = (
        lax.all_gather(coarse_keys, "col", axis=0, tiled=True),
        lax.all_gather(coarse_values, "col", axis=0, tiled=True),
    )
    row_base = lax.axis_index("row") * rows_tiles
    col_base = lax.axis_index("col") * cols_tiles
    rows_total = rows_tiles * lax.axis_size("row")
    cols_total = cols_tiles * lax.axis_size("col")
    windows = []
    usable = []
    for tile_row in range(rows_tiles):
        pieces = []
        kept_list = []
        for row_step in range(3):
            for col_step in range(3):
                pieces.append(padded[:, tile_row + row_step, col_step])
                grid_row = row_base + tile_row + row_step - 1
                grid_col = col_base + 0 + col_step - 1
                inside = (
                    (grid_row >= 0)
                    & (grid_row < rows_total)
                    & (grid_col >= 0)
                    & (grid_col < cols_total)
                )
                kept_here = (keep_flags[tile_row, 0, row_step * 3 + col_step] > 0) | (
                    row_step == 1 and col_step == 1
                )
                kept_list.append(inside & kept_here)
        windows.append(jnp.concatenate(pieces, axis=1))
        usable.append(jnp.stack(kept_list))
    window_kv = jnp.stack(windows, 1)
    window_ok = jnp.repeat(jnp.stack(usable), tile_len, axis=1)
    query_flat = queries.reshape(tile_count, tile_len, model_width)

    def one_head(head):
        begin_at = head * HEAD_DIM
        query_head = lax.dynamic_slice_in_dim(query_flat, begin_at, HEAD_DIM, 2)
        near_keys = lax.dynamic_slice_in_dim(window_kv[0], begin_at, HEAD_DIM, 2)
        near_values = lax.dynamic_slice_in_dim(window_kv[1], begin_at, HEAD_DIM, 2)
        far_key_head = lax.dynamic_slice_in_dim(far_keys, begin_at, HEAD_DIM, 1)
        far_value_head = lax.dynamic_slice_in_dim(far_values, begin_at, HEAD_DIM, 1)
        near_scores = (
            jnp.einsum("tqd,tkd->tqk", query_head, near_keys, preferred_element_type=jnp.float32)
            * scale
        )
        near_scores = jnp.where(window_ok[:, None, :], near_scores, -jnp.inf)
        far_scores = (
            jnp.einsum("tqd,kd->tqk", query_head, far_key_head, preferred_element_type=jnp.float32)
            * scale
        )
        largest = jnp.maximum(jnp.max(near_scores, -1), jnp.max(far_scores, -1))[..., None]
        near_probs = jnp.exp(near_scores - largest)
        far_probs = jnp.exp(far_scores - largest)
        total = jnp.sum(near_probs, -1) + jnp.sum(far_probs, -1)
        mixed = jnp.einsum(
            "tqk,tkd->tqd",
            near_probs.astype(jnp.bfloat16),
            near_values,
            preferred_element_type=jnp.float32,
        )
        mixed = mixed + jnp.einsum(
            "tqk,kd->tqd",
            far_probs.astype(jnp.bfloat16),
            far_value_head,
            preferred_element_type=jnp.float32,
        )
        return mixed / total[..., None]

    result = lax.map(one_head, jnp.arange(HEADS))
    result = jnp.transpose(result, (1, 2, 0, 3)).reshape(
        rows_tiles, cols_tiles, tile_len, model_width
    )
    return result.astype(jnp.bfloat16)


def solution(mesh):
    placed = (
        P("row", "col", None, None),
        P("row", "col", None, None),
        P("row", "col", None, None),
        P("row", "col", None),
        P("col", None),
        P("col", None),
    )
    return jax.shard_map(
        body, mesh=mesh, in_specs=placed, out_specs=P("row", "col", None, None), check_vma=False
    )
```

profile of v0, /device:TPU:31, one launch (start us, length us, event | category | flops | bytes accessed | tf_op | source)
XLA Modules:
  0.0 576.9 jit_solution(1291833222597962540)
XLA Ops:
  8.0 1.7 fusion.29
  9.7 9.4 %collective-permute-start = (bf16[2,1,1,128,2048]{4,3,0,2,1:T(8,128)(2,1)S(1)}, bf16[2,1,1,128,2048]{4,3,0,2,1:T(8,128)(2,1)S(1)}, u32[]{:S(2)}, u32[]{:S(2)}) collective-permute-start(bf16[2,1,1,128,2048]{4,3,0,2,1:T(8,128)(2,1)S(1)} %get-tuple-element.97), channel_id=1, source_target_pairs={{0,16},{16,32},{32,48},{48,64},{64,80},{80,96},{96,112},{112,128},... | collective-permute-start | bytes 3145736 | tf_op jit(solution)/shard_map/ppermute | solution.py:18
  19.1 1.9 collective-permute-start.1
  21.0 42.8 %collective-permute-done = bf16[2,1,1,128,2048]{4,3,0,2,1:T(8,128)(2,1)S(1)} collective-permute-done((bf16[2,1,1,128,2048]{4,3,0,2,1:T(8,128)(2,1)S(1)}, bf16[2,1,1,128,2048]{4,3,0,2,1:T(8,128)(2,1)S(1)}, u32[]{:S(2)}, u32[]{:S(2)}) %collective-permute-start) | collective-permute-done | bytes 1048608 | tf_op jit(solution)/shard_map/ppermute | solution.py:18
  63.8 26.0 %collective-permute-done.1 = bf16[2,1,1,128,2048]{4,3,0,2,1:T(8,128)(2,1)S(1)} collective-permute-done((bf16[2,1,1,128,2048]{4,3,0,2,1:T(8,128)(2,1)S(1)}, bf16[2,1,1,128,2048]{4,3,0,2,1:T(8,128)(2,1)S(1)}, u32[]{:S(2)}, u32[]{:S(2)}) %collective-permute-start.1) | collective-permute-done | bytes 1048608 | tf_op jit(solution)/shard_map/ppermute | solution.py:20
  89.8 3.5 pad_maximum_fusion.1
  93.2 1.9 collective-permute-start.2
  95.2 3.4 collective-permute-start.3
  109.7 135.7 %collective-permute-done.2 = bf16[2,4,1,128,2048]{4,3,0,2,1:T(8,128)(2,1)} collective-permute-done((bf16[2,4,1,128,2048]{4,3,0,2,1:T(8,128)(2,1)}, bf16[2,4,1,128,2048]{4,3,0,2,1:T(8,128)(2,1)}, u32[]{:S(2)}, u32[]{:S(2)}) %collective-permute-start.2) | collective-permute-done | bytes 4194336 | tf_op jit(solution)/shard_map/ppermute | solution.py:18
  248.0 4.7 collective-permute-done.3
  263.4 7.7 %pad_maximum_fusion = bf16[2,2,1152,2048]{3,2,1,0:T(8,128)(2,1)} fusion(bf16[2,1,1152,2048]{3,2,1,0:T(8,128)(2,1)S(1)} %bitcast.140, bf16[2,1,1152,2048]{3,2,1,0:T(8,128)(2,1)S(1)} %bitcast.141), kind=kLoop, calls=%fused_computation.33 | loop fusion | flops 9437184 | bytes 37748736 | tf_op jit(solution)/shard_map/stack | solution.py:63
  271.1 54.0 %all-gather.5.cloned.1.call-done = bf16[2048,2048]{1,0:T(8,128)(2,1)} async-done(((bf16[128,2048]{1,0:T(8,128)(2,1)}), bf16[2048,2048]{1,0:T(8,128)(2,1)}) %all-gather.5.cloned.1.call-update) | async-done | bytes 8388624 | tf_op jit(solution)/shard_map/all_gather | solution.py:35
  325.2 242.9 %while.11 = (s32[]{:T(128)}, bf16[16,2,128,128]{3,2,1,0:T(8,128)(2,1)S(1)}, s32[16]{0:T(128)S(1)}, bf16[2,128,2048]{2,1,0:T(8,128)(2,1)}, bf16[2,2,1152,2048]{3,...) while((s32[]{:T(128)}, ...), condition=%wide.region_5.6_spmd.clone, body=%wide.region_0.5_spmd.clone.sunk | while | flops 424705536 | bytes 50360780 | solution.py:101
  326.4 8.1 %fusion.62 = (bf16[1,2,1152,2048]{3,2,1,0:T(8,128)(2,1)S(1)}, bf16[1,2,1152,2048]{3,2,1,0:T(8,128)(2,1)S(1)}) fusion(bf16[2,2,1152,2048]{3,2,1,0:T(8,128)(2,1)} %get-tuple-element.208), kind=kLoop, calls=%fused_computation.67.clone.1 | loop fusion | bytes 37748736 | tf_op jit(solution)/shard_map/while/body/eval_jaxpr/slice | solution.py:71
  335.9 1.6 fusion.61
  341.6 8.1 %fusion.62 = (bf16[1,2,1152,2048]{3,2,1,0:T(8,128)(2,1)S(1)}, bf16[1,2,1152,2048]{3,2,1,0:T(8,128)(2,1)S(1)}) fusion(bf16[2,2,1152,2048]{3,2,1,0:T(8,128)(2,1)} %get-tuple-element.208), kind=kLoop, calls=%fused_computation.67.clone.1 | loop fusion | bytes 37748736 | tf_op jit(solution)/shard_map/while/body/eval_jaxpr/slice | solution.py:71
  356.8 8.1 %fusion.62 = (bf16[1,2,1152,2048]{3,2,1,0:T(8,128)(2,1)S(1)}, bf16[1,2,1152,2048]{3,2,1,0:T(8,128)(2,1)S(1)}) fusion(bf16[2,2,1152,2048]{3,2,1,0:T(8,128)(2,1)} %get-tuple-element.208), kind=kLoop, calls=%fused_computation.67.clone.1 | loop fusion | bytes 37748736 | tf_op jit(solution)/shard_map/while/body/eval_jaxpr/slice | solution.py:71
  372.0 8.1 %fusion.62 = (bf16[1,2,1152,2048]{3,2,1,0:T(8,128)(2,1)S(1)}, bf16[1,2,1152,2048]{3,2,1,0:T(8,128)(2,1)S(1)}) fusion(bf16[2,2,1152,2048]{3,2,1,0:T(8,128)(2,1)} %get-tuple-element.208), kind=kLoop, calls=%fused_computation.67.clone.1 | loop fusion | bytes 37748736 | tf_op jit(solution)/shard_map/while/body/eval_jaxpr/slice | solution.py:71
  381.5 1.6 fusion.61
  387.2 8.1 %fusion.62 = (bf16[1,2,1152,2048]{3,2,1,0:T(8,128)(2,1)S(1)}, bf16[1,2,1152,2048]{3,2,1,0:T(8,128)(2,1)S(1)}) fusion(bf16[2,2,1152,2048]{3,2,1,0:T(8,128)(2,1)} %get-tuple-element.208), kind=kLoop, calls=%fused_computation.67.clone.1 | loop fusion | bytes 37748736 | tf_op jit(solution)/shard_map/while/body/eval_jaxpr/slice | solution.py:71
  402.4 8.1 %fusion.62 = (bf16[1,2,1152,2048]{3,2,1,0:T(8,128)(2,1)S(1)}, bf16[1,2,1152,2048]{3,2,1,0:T(8,128)(2,1)S(1)}) fusion(bf16[2,2,1152,2048]{3,2,1,0:T(8,128)(2,1)} %get-tuple-element.208), kind=kLoop, calls=%fused_computation.67.clone.1 | loop fusion | bytes 37748736 | tf_op jit(solution)/shard_map/while/body/eval_jaxpr/slice | solution.py:71
  417.5 8.1 %fusion.62 = (bf16[1,2,1152,2048]{3,2,1,0:T(8,128)(2,1)S(1)}, bf16[1,2,1152,2048]{3,2,1,0:T(8,128)(2,1)S(1)}) fusion(bf16[2,2,1152,2048]{3,2,1,0:T(8,128)(2,1)} %get-tuple-element.208), kind=kLoop, calls=%fused_computation.67.clone.1 | loop fusion | bytes 37748736 | tf_op jit(solution)/shard_map/while/body/eval_jaxpr/slice | solution.py:71
  432.7 8.1 %fusion.62 = (bf16[1,2,1152,2048]{3,2,1,0:T(8,128)(2,1)S(1)}, bf16[1,2,1152,2048]{3,2,1,0:T(8,128)(2,1)S(1)}) fusion(bf16[2,2,1152,2048]{3,2,1,0:T(8,128)(2,1)} %get-tuple-element.208), kind=kLoop, calls=%fused_computation.67.clone.1 | loop fusion | bytes 37748736 | tf_op jit(solution)/shard_map/while/body/eval_jaxpr/slice | solution.py:71
  447.9 8.1 %fusion.62 = (bf16[1,2,1152,2048]{3,2,1,0:T(8,128)(2,1)S(1)}, bf16[1,2,1152,2048]{3,2,1,0:T(8,128)(2,1)S(1)}) fusion(bf16[2,2,1152,2048]{3,2,1,0:T(8,128)(2,1)} %get-tuple-element.208), kind=kLoop, calls=%fused_computation.67.clone.1 | loop fusion | bytes 37748736 | tf_op jit(solution)/shard_map/while/body/eval_jaxpr/slice | solution.py:71
  457.4 1.6 fusion.61
  463.1 8.1 %fusion.62 = (bf16[1,2,1152,2048]{3,2,1,0:T(8,128)(2,1)S(1)}, bf16[1,2,1152,2048]{3,2,1,0:T(8,128)(2,1)S(1)}) fusion(bf16[2,2,1152,2048]{3,2,1,0:T(8,128)(2,1)} %get-tuple-element.208), kind=kLoop, calls=%fused_computation.67.clone.1 | loop fusion | bytes 37748736 | tf_op jit(solution)/shard_map/while/body/eval_jaxpr/slice | solution.py:71
  478.3 8.1 %fusion.62 = (bf16[1,2,1152,2048]{3,2,1,0:T(8,128)(2,1)S(1)}, bf16[1,2,1152,2048]{3,2,1,0:T(8,128)(2,1)S(1)}) fusion(bf16[2,2,1152,2048]{3,2,1,0:T(8,128)(2,1)} %get-tuple-element.208), kind=kLoop, calls=%fused_computation.67.clone.1 | loop fusion | bytes 37748736 | tf_op jit(solution)/shard_map/while/body/eval_jaxpr/slice | solution.py:71
  493.5 8.1 %fusion.62 = (bf16[1,2,1152,2048]{3,2,1,0:T(8,128)(2,1)S(1)}, bf16[1,2,1152,2048]{3,2,1,0:T(8,128)(2,1)S(1)}) fusion(bf16[2,2,1152,2048]{3,2,1,0:T(8,128)(2,1)} %get-tuple-element.208), kind=kLoop, calls=%fused_computation.67.clone.1 | loop fusion | bytes 37748736 | tf_op jit(solution)/shard_map/while/body/eval_jaxpr/slice | solution.py:71
  508.6 8.1 %fusion.62 = (bf16[1,2,1152,2048]{3,2,1,0:T(8,128)(2,1)S(1)}, bf16[1,2,1152,2048]{3,2,1,0:T(8,128)(2,1)S(1)}) fusion(bf16[2,2,1152,2048]{3,2,1,0:T(8,128)(2,1)} %get-tuple-element.208), kind=kLoop, calls=%fused_computation.67.clone.1 | loop fusion | bytes 37748736 | tf_op jit(solution)/shard_map/while/body/eval_jaxpr/slice | solution.py:71
  523.8 8.1 %fusion.62 = (bf16[1,2,1152,2048]{3,2,1,0:T(8,128)(2,1)S(1)}, bf16[1,2,1152,2048]{3,2,1,0:T(8,128)(2,1)S(1)}) fusion(bf16[2,2,1152,2048]{3,2,1,0:T(8,128)(2,1)} %get-tuple-element.208), kind=kLoop, calls=%fused_computation.67.clone.1 | loop fusion | bytes 37748736 | tf_op jit(solution)/shard_map/while/body/eval_jaxpr/slice | solution.py:71
  539.0 8.1 %fusion.62 = (bf16[1,2,1152,2048]{3,2,1,0:T(8,128)(2,1)S(1)}, bf16[1,2,1152,2048]{3,2,1,0:T(8,128)(2,1)S(1)}) fusion(bf16[2,2,1152,2048]{3,2,1,0:T(8,128)(2,1)} %get-tuple-element.208), kind=kLoop, calls=%fused_computation.67.clone.1 | loop fusion | bytes 37748736 | tf_op jit(solution)/shard_map/while/body/eval_jaxpr/slice | solution.py:71
  554.2 8.1 %fusion.62 = (bf16[1,2,1152,2048]{3,2,1,0:T(8,128)(2,1)S(1)}, bf16[1,2,1152,2048]{3,2,1,0:T(8,128)(2,1)S(1)}) fusion(bf16[2,2,1152,2048]{3,2,1,0:T(8,128)(2,1)} %get-tuple-element.208), kind=kLoop, calls=%fused_computation.67.clone.1 | loop fusion | bytes 37748736 | tf_op jit(solution)/shard_map/while/body/eval_jaxpr/slice | solution.py:71
  (204 shorter events, 114.5 us)
Async XLA Ops:
  6.5 92.0 %copy-start.2 = (s32[2,1,9]{2,1,0:T(1,128)S(1)}, s32[2,1,9]{2,1,0:T(1,128)}, u32[]{:S(2)}) copy-start(s32[2,1,9]{2,1,0:T(1,128)} %param.11) | copy-start | bytes 220
  6.5 264.6 %all-gather.3.cloned.1.call-start = ((), (), s32[]{:S(2)}) async-start(), calls=%async_computation | async-start | bytes 8912896 | tf_op jit(solution)/shard_map/all_gather | solution.py:34
  7.3 317.9 %all-gather.5.cloned.1.call-start = ((), (), s32[]{:S(2)}) async-start(), calls=%async_computation.1 | async-start | bytes 8912896 | tf_op jit(solution)/shard_map/all_gather | solution.py:35
  9.7 54.1 %collective-permute-start = (bf16[2,1,1,128,2048]{4,3,0,2,1:T(8,128)(2,1)S(1)}, bf16[2,1,1,128,2048]{4,3,0,2,1:T(8,128)(2,1)S(1)}, u32[]{:S(2)}, u32[]{:S(2)}) collective-permute-start(bf16[2,1,1,128,2048]{4,3,0,2,1:T(8,128)(2,1)S(1)} %get-tuple-element.97), channel_id=1, source_target_pairs={{0,16},{16,32},{32,48},{48,64},{64,80},{80,96},{96,112},{112,128},... | collective-permute-start | bytes 3145736 | tf_op jit(solution)/shard_map/ppermute | solution.py:18
  19.1 70.7 %collective-permute-start.1 = (bf16[2,1,1,128,2048]{4,3,0,2,1:T(8,128)(2,1)S(1)}, bf16[2,1,1,128,2048]{4,3,0,2,1:T(8,128)(2,1)S(1)}, u32[]{:S(2)}, u32[]{:S(2)}) collective-permute-start(bf16[2,1,1,128,2048]{4,3,0,2,1:T(8,128)(2,1)S(1)} %get-tuple-element.98), channel_id=1, source_target_pairs={{16,0},{32,16},{48,32},{64,48},{80,64},{96,80},{112,96},{128,112},... | collective-permute-start | bytes 3145736 | tf_op jit(solution)/shard_map/ppermute | solution.py:20
  63.8 26.0 %copy-start = (bf16[2,1,1,128,2048]{4,3,0,2,1:T(8,128)(2,1)}, bf16[2,1,1,128,2048]{4,3,0,2,1:T(8,128)(2,1)S(1)}, u32[]{:S(2)}) copy-start(bf16[2,1,1,128,2048]{4,3,0,2,1:T(8,128)(2,1)S(1)} %collective-permute-done) | copy-start | bytes 3145732
  93.2 152.2 %collective-permute-start.2 = (bf16[2,4,1,128,2048]{4,3,0,2,1:T(8,128)(2,1)}, bf16[2,4,1,128,2048]{4,3,0,2,1:T(8,128)(2,1)}, u32[]{:S(2)}, u32[]{:S(2)}) collective-permute-start(bf16[2,4,1,128,2048]{4,3,0,2,1:T(8,128)(2,1)} %pad_maximum_fusion.1), channel_id=1, source_target_pairs={{0,1},{1,2},{2,3},{3,4},{4,5},{5,6},{6,7},{7,8},{8,9},{9,10},{10,1... | collective-permute-start | bytes 12582920 | tf_op jit(solution)/shard_map/ppermute | solution.py:18
  95.2 157.5 %collective-permute-start.3 = (bf16[2,4,1,128,2048]{4,3,0,2,1:T(8,128)(2,1)}, bf16[2,4,1,128,2048]{4,3,0,2,1:T(8,128)(2,1)}, u32[]{:S(2)}, u32[]{:S(2)}) collective-permute-start(bf16[2,4,1,128,2048]{4,3,0,2,1:T(8,128)(2,1)} %pad_maximum_fusion.1), channel_id=1, source_target_pairs={{1,0},{2,1},{3,2},{4,3},{5,4},{6,5},{7,6},{8,7},{9,8},{10,9},{11,1... | collective-permute-start | bytes 12582920 | tf_op jit(solution)/shard_map/ppermute | solution.py:20
  263.4 61.8 %copy-start.1 = (bf16[16,2,128,128]{3,2,1,0:T(8,128)(2,1)S(1)}, bf16[16,2,128,128]{3,2,1,0:T(8,128)(2,1)}, u32[]{:S(2)}) copy-start(bf16[16,2,128,128]{3,2,1,0:T(8,128)(2,1)} %custom-call.2) | copy-start | bytes 3145732
Sparse Core Ops, SparseCore 0:
  9.1 190.6 all-gather.2
  201.6 123.4 all-gather.4
where the time goes:
time: 582 us; the launch traced here: 577 us
  waiting for transfers between devices  265 us (46%)
  local copies, waits for them, and re-layouts  157 us (27%)
  matrix products  78.3 us (13%)
  other arithmetic  25.5 us (4%)
  between operations  23.8 us (4%)
  starting transfers between devices  16.6 us (3%)
  loops' own time  11.2 us (2%)
    ppermute x2, waiting for transfers between devices, padded_2(): lax.ppermute(tail, axis, [(i, (i + 1) % count) for i in range(ends)])  178 us
    slice x16, local copies, waits for them, and re-layouts, one_head(): near_values = lax.dynamic_slice_in_dim(window_kv[1], begin_at, HEAD_DIM, 2)  130 us
    all_gather x1, waiting for transfers between devices, body(): lax.all_gather(coarse_values, 'col', axis=0, tiled=True)  54 us
    ppermute x2, waiting for transfers between devices, padded_2(): lax.ppermute(head, axis, [((i + 1) % count, i) for i in range(ends)])  30.7 us
    dot_general x16, matrix products, one_head(): jnp.einsum('tqd,kd->tqk', query_head, far_key_head, preferred_element_typ...  25.6 us
    dot_general x16, matrix products, one_head(): jnp.einsum('tqk,kd->tqd', far_probs.astype(jnp.bfloat16), far_value_head,...  25 us
    dot_general x16, matrix products, one_head(): jnp.einsum('tqd,tkd->tqk', query_head, near_keys, preferred_element_type=...  20.5 us
    reduce_sum x32, other arithmetic, one_head(): total = jnp.sum(near_probs, -1) + jnp.sum(far_probs, -1)  12.4 us
  transfers between devices with their start and end apart: 6, of which 5 were waited for; matrix products, arithmetic and copies ran while one was open for 5% of the time, Pallas kernels for 0%

commit v1 on v0

v1 whole, which is shorter than its diff:
```python
import jax
import jax.numpy as jnp
from jax import lax
from jax.experimental import pallas as pl
from jax.experimental.pallas import tpu as pltpu
from jax.sharding import PartitionSpec as P

HEAD_DIM = 128
NX, NY, NZ = 4, 4, 8
ZL = 4
PAIR = 256
LOG2E = 1.4426950408889634
MESH = pl.DeviceIdType.MESH

KE, VE, KI, VI, QQ, BB, CK, CV = 0, 8, 16, 24, 32, 40, 48, 52
CK2, CV2 = 56, 60
CK3, CV3 = 64, 80
RK, RV = 96, 104
HK, HV = 112, 114
XK, XV = 116, 120
OI, OE = 124, 132
SEMS = 140


def kernel(q_hbm, k_hbm, v_hbm, bias_hbm, ck_hbm, cv_hbm, out_hbm,
           qb, kb, vb, bb, ckb, cvb, ob, acc, mst, lst, ss, rs):
    row = lax.axis_index("row")
    col = lax.axis_index("col")
    core = lax.rem(row, 2)
    pair = row // 2
    zh = lax.rem(pair, 2)
    y = pair // 2
    x = lax.rem(col, NX)
    zl = col // NX
    z = zh * ZL + zl
    group = x * 2 + core

    def at(x_, y_, z_, c_):
        return ((y_ * 2 + z_ // ZL) * 2 + c_, lax.rem(z_, ZL) * NX + x_)

    def along_x(dx, dc):
        return at(lax.rem(x + dx, NX), y, z, lax.rem(core + dc, 2))

    def along_y(dy):
        return at(x, lax.rem(y + dy, NY), z, core)

    def along_z(dz):
        return at(x, y, lax.rem(z + dz + NZ, NZ), core)

    def along_p(dp):
        return (lax.rem(pair + dp + 8, 8) * 2 + core, col)

    mates = [(dx, dc) for dx in range(NX) for dc in range(2) if dx or dc]
    peers = [along_x(dx, dc) for dx, dc in mates]
    peers += [along_y(d) for d in (1, 2, 3)]
    peers += [along_z(d) for d in (1, -1, 2, -2)]
    peers += [along_p(d) for d in (1, -1)]
    barrier = pltpu.get_barrier_semaphore()
    for peer in peers:
        pl.semaphore_signal(barrier, inc=1, device_id=peer, device_id_type=MESH)

    sent = []
    kept = []

    def keep(src, dst, sem):
        copy = pltpu.make_async_copy(src, dst, rs.at[sem])
        copy.start()
        kept.append(copy)

    def send(src, dst, sem, peer):
        copy = pltpu.make_async_remote_copy(
            src_ref=src, dst_ref=dst, send_sem=ss.at[sem], recv_sem=rs.at[sem],
            device_id=peer, device_id_type=MESH)
        copy.start()
        sent.append(copy)

    def arrived(dst, sem):
        pltpu.make_async_copy(dst, dst, rs.at[sem]).wait()

    def lanes(g):
        return pl.ds(pl.multiple_of(g * PAIR, PAIR), PAIR)

    edge_row = 1 + 3 * core
    inner_row = 2 + core
    quarter = pl.ds(pl.multiple_of(y * 32, 32), 32)

    mine = lanes(group)
    keep(k_hbm.at[core, 0, :, mine], kb.at[edge_row, 1 + x], KE)
    keep(v_hbm.at[core, 0, :, mine], vb.at[edge_row, 1 + x], VE)
    keep(ck_hbm.at[quarter, mine], ckb.at[y, zl, x], CK)
    keep(cv_hbm.at[quarter, mine], cvb.at[y, zl, x], CV)
    keep(k_hbm.at[1 - core, 0, :, mine], kb.at[inner_row, 1 + x], KI)
    keep(v_hbm.at[1 - core, 0, :, mine], vb.at[inner_row, 1 + x], VI)
    keep(q_hbm.at[:, 0, :, mine], qb.at[pl.ds(2 * core, 2), x], QQ)
    keep(bias_hbm, bb.at[pl.ds(2 * core, 2), x], BB)

    pl.semaphore_wait(barrier, len(peers))

    for dx, dc in mates:
        cols = lanes(lax.rem(x + dx, NX) * 2 + lax.rem(core + dc, 2))
        send(k_hbm.at[core, 0, :, cols], kb.at[edge_row, 1 + x], KE + dx * 2 + dc, along_x(dx, dc))
        send(v_hbm.at[core, 0, :, cols], vb.at[edge_row, 1 + x], VE + dx * 2 + dc, along_x(dx, dc))
    for dx in (1, 2, 3):
        cols = lanes(lax.rem(x + dx, NX) * 2 + core)
        send(ck_hbm.at[quarter, cols], ckb.at[y, zl, x], CK + dx, along_x(dx, 0))
        send(cv_hbm.at[quarter, cols], cvb.at[y, zl, x], CV + dx, along_x(dx, 0))
    for dx, dc in mates:
        cols = lanes(lax.rem(x + dx, NX) * 2 + lax.rem(core + dc, 2))
        send(k_hbm.at[1 - core, 0, :, cols], kb.at[inner_row, 1 + x], KI + dx * 2 + dc, along_x(dx, dc))
        send(v_hbm.at[1 - core, 0, :, cols], vb.at[inner_row, 1 + x], VI + dx * 2 + dc, along_x(dx, dc))
    for dx, dc in mates:
        cols = lanes(lax.rem(x + dx, NX) * 2 + lax.rem(core + dc, 2))
        send(q_hbm.at[:, 0, :, cols], qb.at[pl.ds(2 * core, 2), x], QQ + dx * 2 + dc, along_x(dx, dc))
        send(bias_hbm, bb.at[pl.ds(2 * core, 2), x], BB + dx * 2 + dc, along_x(dx, dc))

    for j in (0, 3, 1, 2):
        dx = lax.rem(x + NX - j, NX)
        for top in (0, 1):
            dc = lax.rem(core + top, 2)
            src_row, dst_row, peer = ((1, 5, along_p(-1)), (4, 0, along_p(1)))[top]
            arrived(kb.at[src_row, 1 + j], KE + dx * 2 + dc)
            send(kb.at[src_row, 1 + j], kb.at[dst_row, 1 + j], RK + top * 4 + j, peer)
            arrived(vb.at[src_row, 1 + j], VE + dx * 2 + dc)
            send(vb.at[src_row, 1 + j], vb.at[dst_row, 1 + j], RV + top * 4 + j, peer)

    for buf, first, second, far in ((ckb, CK, CK2, 2), (cvb, CV, CV2, -2)):
        for dx in range(NX):
            arrived(buf.at[y, zl, lax.rem(x + NX - dx, NX)], first + dx)
        send(buf.at[y, zl], buf.at[y, zl], second + 1, along_z(1))
        send(buf.at[y, zl], buf.at[y, zl], second + 3, along_z(-1))
        send(buf.at[y, zl], buf.at[y, zl], second + 2, along_z(far))

    for dx in range(NX):
        j = lax.rem(x + NX - dx, NX)
        for s in (0, 1):
            dc = lax.rem(core + s, 2)
            arrived(kb.at[2 + s, 1 + j], KI + dx * 2 + dc)
            arrived(vb.at[2 + s, 1 + j], VI + dx * 2 + dc)
    for buf, sem in ((kb, HK), (vb, HV)):
        send(buf.at[pl.ds(1, 4), 4], buf.at[pl.ds(1, 4), 0], sem, along_z(1))
        send(buf.at[pl.ds(1, 4), 1], buf.at[pl.ds(1, 4), 5], sem + 1, along_z(-1))

    for dz in (0, 1, 3, 2):
        from_zl = lax.rem(zl + ZL - dz, ZL)
        for buf, second, third in ((ckb, CK2, CK3), (cvb, CV2, CV3)):
            if dz:
                arrived(buf.at[y, from_zl], second + dz)
            for dy in (1, 2, 3):
                send(buf.at[y, from_zl], buf.at[y, from_zl], third + dz * 4 + dy, along_y(dy))

    for dx in range(NX):
        j = lax.rem(x + NX - dx, NX)
        for dc in (0, 1):
            half = pl.ds(2 * lax.rem(core + dc, 2), 2)
            arrived(qb.at[half, j], QQ + dx * 2 + dc)
            arrived(bb.at[half, j], BB + dx * 2 + dc)
    for buf, sem in ((kb, HK), (vb, HV)):
        arrived(buf.at[pl.ds(1, 4), 0], sem)
        arrived(buf.at[pl.ds(1, 4), 5], sem + 1)
    for dz in range(ZL):
        from_zl = lax.rem(zl + ZL - dz, ZL)
        for buf, third in ((ckb, CK3), (cvb, CV3)):
            for dy in (1, 2, 3):
                arrived(buf.at[lax.rem(y + NY - dy, NY), from_zl], third + dz * 4 + dy)

    factor = LOG2E * HEAD_DIM ** -0.5
    contract = (((1,), (1,)), ((), ()))

    def near(i, j, h, a):
        heads = slice(h * HEAD_DIM, (h + 1) * HEAD_DIM)
        keys = kb[i + a, pl.ds(j, 3), :, heads].reshape(3 * 128, HEAD_DIM)
        values = vb[i + a, pl.ds(j, 3), :, heads].reshape(3 * 128, HEAD_DIM)
        return keys, values, bb[i, j, a:a + 1, :]

    def attend(i, j, h, rows, coarse):
        heads = slice(h * HEAD_DIM, (h + 1) * HEAD_DIM)
        query = qb[i, j, :, heads]
        scores, values = [], []
        for a in rows:
            keys, vals, bias = near(i, j, h, a)
            scores.append(lax.dot_general(query, keys, contract, preferred_element_type=jnp.float32) + bias)
            values.append(vals)
        if coarse:
            keys = ckb[:, :, :, :, heads].reshape(2048, HEAD_DIM)
            scores.append(lax.dot_general(query, keys, contract, preferred_element_type=jnp.float32))
            values.append(cvb[:, :, :, :, heads].reshape(2048, HEAD_DIM))
        return scores, values

    def combine(scores, values, floor):
        largest = scores[0].max(-1, keepdims=True)
        for s in scores[1:]:
            largest = jnp.maximum(largest, s.max(-1, keepdims=True))
        if floor is not None:
            largest = jnp.maximum(largest, floor)
        total, mixed = None, None
        shift = largest * factor
        for s, v in zip(scores, values):
            p = jnp.exp2(s * factor - shift)
            t = p.sum(-1, keepdims=True)
            o = jnp.dot(p.astype(jnp.bfloat16), v, preferred_element_type=jnp.float32)
            total = t if total is None else total + t
            mixed = o if mixed is None else mixed + o
        return largest, total, mixed

    def give_back(out_sem, source_row, tile_of):
        for dx in range(NX):
            for dc in (0, 1):
                to_x = lax.rem(x + dx, NX)
                to_c = lax.rem(core + dc, 2)
                src = ob.at[source_row(to_c), to_x]
                dst = out_hbm.at[tile_of(to_c), 0, :, mine]
                if dx or dc:
                    send(src, dst, out_sem + dx * 2 + dc, along_x(dx, dc))
                else:
                    keep(src, dst, out_sem)

    def get_back(out_sem, tile):
        for dx in range(NX):
            for dc in (0, 1):
                g = lax.rem(x + NX - dx, NX) * 2 + lax.rem(core + dc, 2)
                arrived(out_hbm.at[tile, 0, :, lanes(g)], out_sem + dx * 2 + dc)

    @pl.loop(0, 8)
    def _(t):
        i, j = 1 + t // 4, lax.rem(t, 4)
        for h in (0, 1):
            scores, values = attend(i, j, h, (0, 1, 2), True)
            _, total, mixed = combine(scores, values, None)
            ob[i, j, :, h * HEAD_DIM:(h + 1) * HEAD_DIM] = (mixed / total).astype(jnp.bfloat16)

    give_back(OI, lambda c: 1 + c, lambda c: 1 - c)

    for j, src_col, dst_col, dz, which in ((3, 4, 0, 1, 0), (0, 1, 5, -1, 1)):
        for top, r in ((0, 5), (1, 0)):
            for buf, rsem, xsem in ((kb, RK, XK), (vb, RV, XV)):
                arrived(buf.at[r, src_col], rsem + top * 4 + j)
                send(buf.at[r, src_col], buf.at[r, dst_col], xsem + which * 2 + top, along_z(dz))

    for i, rows in ((0, (1, 2)), (3, (0, 1))):
        @pl.loop(0, 4)
        def _(j):
            for h in (0, 1):
                scores, values = attend(i, j, h, rows, True)
                largest, total, mixed = combine(scores, values, None)
                at_ = (i // 3) * 4 + j
                acc[h, at_] = mixed
                mst[h, at_] = jnp.broadcast_to(largest, (128, 128))
                lst[h, at_] = jnp.broadcast_to(total, (128, 128))

    for top, r in ((0, 5), (1, 0)):
        for buf, rsem, xsem in ((kb, RK, XK), (vb, RV, XV)):
            for j in (1, 2):
                arrived(buf.at[r, 1 + j], rsem + top * 4 + j)
            arrived(buf.at[r, 0], xsem + top)
            arrived(buf.at[r, 5], xsem + 2 + top)

    for i, a in ((0, 0), (3, 2)):
        @pl.loop(0, 4)
        def _(j):
            for h in (0, 1):
                at_ = (i // 3) * 4 + j
                scores, values = attend(i, j, h, (a,), False)
                before = mst[h, at_]
                largest, total, mixed = combine(scores, values, before[:, :1])
                scale = jnp.exp2((before - largest) * factor)
                mixed = mixed + acc[h, at_] * scale
                total = total + lst[h, at_] * scale
                ob[i, j, :, h * HEAD_DIM:(h + 1) * HEAD_DIM] = (mixed / total).astype(jnp.bfloat16)

    give_back(OE, lambda c: 3 * c, lambda c: c)
    get_back(OI, 1 - core)
    get_back(OE, core)
    for copy in sent:
        copy.wait_send()


def body(queries, fine_keys, fine_values, keep_flags, coarse_keys, coarse_values):
    rows_tiles = queries.shape[0]
    steps = jnp.arange(3) - 1
    grid_row = lax.axis_index("row") * rows_tiles + jnp.arange(rows_tiles)[:, None, None] + steps[None, :, None]
    grid_col = lax.axis_index("col") + steps[None, None, :]
    inside = (grid_row >= 0) & (grid_row < rows_tiles * lax.axis_size("row"))
    inside = inside & (grid_col >= 0) & (grid_col < lax.axis_size("col"))
    own = (steps[:, None] == 0) & (steps[None, :] == 0)
    usable = inside & ((keep_flags.reshape(rows_tiles, 3, 3) > 0) | own[None])
    bias = jnp.where(usable, 0.0, -jnp.inf).astype(jnp.float32)
    bias = jnp.broadcast_to(bias[..., None], (rows_tiles, 3, 3, 128)).reshape(rows_tiles, 3, 384)
    bias = jnp.pad(bias, ((0, 0), (0, 5), (0, 0)))
    bf16, f32 = jnp.bfloat16, jnp.float32
    return pl.pallas_call(
        kernel,
        out_shape=jax.ShapeDtypeStruct(queries.shape, bf16),
        in_specs=[pl.BlockSpec(memory_space=pl.ANY)] * 6,
        out_specs=pl.BlockSpec(memory_space=pl.ANY),
        scratch_shapes=[
            pltpu.VMEM((4, 4, 128, PAIR), bf16),
            pltpu.VMEM((6, 6, 128, PAIR), bf16),
            pltpu.VMEM((6, 6, 128, PAIR), bf16),
            pltpu.VMEM((4, 4, 8, 384), f32),
            pltpu.VMEM((NY, ZL, NX, 32, PAIR), bf16),
            pltpu.VMEM((NY, ZL, NX, 32, PAIR), bf16),
            pltpu.VMEM((4, 4, 128, PAIR), bf16),
            pltpu.VMEM((2, 8, 128, 128), f32),
            pltpu.VMEM((2, 8, 128, 128), f32),
            pltpu.VMEM((2, 8, 128, 128), f32),
            pltpu.SemaphoreType.DMA((SEMS,)),
            pltpu.SemaphoreType.DMA((SEMS,)),
        ],
        compiler_params=pltpu.CompilerParams(
            collective_id=0, has_side_effects=True, vmem_limit_bytes=48 << 20),
        name="window_attention",
    )(queries, fine_keys, fine_values, bias, coarse_keys, coarse_values)


def solution(mesh):
    placed = (
        P("row", "col", None, None),
        P("row", "col", None, None),
        P("row", "col", None, None),
        P("row", "col", None),
        P("col", None),
        P("col", None),
    )
    return jax.shard_map(
        body, mesh=mesh, in_specs=placed, out_specs=P("row", "col", None, None), check_vma=False
    )
```

time: 582 us -> 143 us (0.25)
  the two profiles are of different devices: /device:TPU:31 before, /device:TPU:1 now
where the time goes in v1:
time: 143 us
  Pallas kernels  135 us (94%)
  local copies, waits for them, and re-layouts  7.6 us (5%)
    pallas_call x1, Pallas kernels, body(): pl.pallas_call(kernel, out_shape=jax.ShapeDtypeStruct(queries.shape, bf16...  135 us
    unnamed x13, local copies, waits for them, and re-layouts  7.4 us

profile of v1, /device:TPU:1, one launch (start us, length us, event | category | flops | bytes accessed | tf_op | source)
XLA Modules:
  0.0 142.6 jit_solution(3018399344165826628)
XLA Ops:
  0.0 0.0 copy-start.5
  0.0 0.7 copy-done.5
  0.7 0.1 gt.11
  0.8 0.1 broadcast_and_fusion
  0.9 0.1 compare_and_fusion
  1.0 0.1 and_select_fusion
  1.0 0.1 broadcast_in_dim.12
  1.2 0.0 copy-start
  1.2 1.2 copy-done
  2.4 0.0 copy-start.1
  2.4 1.2 copy-done.1
  3.6 0.0 copy-start.2
  3.6 1.2 copy-done.2
  4.9 0.0 copy-start.3
  4.9 1.0 copy-done.3
  5.9 0.0 copy-start.4
  5.9 1.0 copy-done.4
  6.9 134.7 %window_attention.1 = bf16[2,1,128,2048]{3,2,1,0:T(8,128)(2,1)S(1)} custom-call(bf16[2,1,128,2048]{3,2,1,0:T(8,128)(2,1)S(1)} %copy-done, bf16[2,1,128,2048]{3,2,1,0:T(8,128)(2,1)S(1)} %copy-done.1, bf16[2,1,128,2048]{3,2,1,0:T(8,128)(2,1)S(1)} %copy-done.2, f32[2,8,384]{2,1,0:T(8,128)S(1)} %pad.4.bias_hbm, bf16[128,2048]{1,0:T(8,128)(2,1)S(1)} %copy-done.3, ...), custom_call_target="tpu_custom_call" | custom-call | tf_op jit(solution)/shard_map/window_attention/pallas_call | solution.py:290
  141.6 1.0 copy.10
  (9 shorter events, 0.1 us)
Async XLA Ops:
  0.0 0.7 copy-start.5
  1.2 1.2 copy-start
  2.4 1.2 copy-start.1
  3.6 1.2 copy-start.2
  4.9 1.0 copy-start.3
  5.9 1.0 copy-start.4

commit v2 on v1

v2 whole, which is shorter than its diff:
```python
import jax
import jax.numpy as jnp
from jax import lax
from jax.experimental import pallas as pl
from jax.experimental.pallas import tpu as pltpu
from jax.sharding import PartitionSpec as P

HEAD_DIM = 128
NX, NY, NZ = 4, 4, 8
ZL = 4
NP = 8
PAIR = 256
LOG2E = 1.4426950408889634
MESH = pl.DeviceIdType.MESH

KE, VE, KI, VI, QQ, BB = 0, 8, 16, 24, 32, 40
CZK, CZV = 48, 52
CXK, CXV = 56, 60
CYK, CYV = 64, 68
RK, RV = 72, 84
HK, HV = 96, 98
OI, OE = 100, 108
FLAGS = 116
SEMS = 117


def kernel(q_hbm, k_hbm, v_hbm, flags_hbm, ck_hbm, cv_hbm, out_hbm,
           qb, kb, vb, flags, bias, bb, zk, zv, ckb, cvb, ob, acc, mst, lst, ss, rs):
    row = lax.axis_index("row")
    col = lax.axis_index("col")
    core = lax.rem(row, 2)
    pair = row // 2
    zh = lax.rem(pair, 2)
    y = pair // 2
    x = lax.rem(col, NX)
    zl = col // NX
    z = zh * ZL + zl

    def at(x_, y_, z_, c_):
        return ((y_ * 2 + z_ // ZL) * 2 + c_, lax.rem(z_, ZL) * NX + x_)

    def along_x(dx, dc):
        return at(lax.rem(x + dx, NX), y, z, lax.rem(core + dc, 2))

    def along_y(dy):
        return at(x, lax.rem(y + dy, NY), z, core)

    def along_z(dz):
        return at(x, y, lax.rem(z + dz + NZ, NZ), core)

    def halo_target(dp, dz):
        band = lax.rem(pair + dp + NP, NP)
        z_ = lax.rem(lax.rem(band, 2) * ZL + zl + dz + NZ, NZ)
        return at(x, band // 2, z_, core)

    def halo_source(dp, dz):
        z_ = lax.rem(z - dz + NZ, NZ)
        band = lax.rem(y * 2 + z_ // ZL - dp + NP, NP)
        return (band * 2 + core, lax.rem(z_, ZL) * NX + x)

    mates = [(dx, dc) for dx in (0, 1, 3, 2) for dc in (1, 0) if dx or dc]
    callers = [along_x(dx, dc) for dx, dc in mates]
    callers += [along_y(d) for d in (1, 2, 3)]
    callers += [along_z(d) for d in (1, -1, 2, -2)]
    callers += [halo_source(dp, dz) for dp in (1, -1) for dz in (-1, 0, 1)]
    barrier = pltpu.get_barrier_semaphore()
    for peer in callers:
        pl.semaphore_signal(barrier, inc=1, device_id=peer, device_id_type=MESH)

    sent = []

    def keep(src, dst, sem):
        pltpu.make_async_copy(src, dst, rs.at[sem]).start()

    def send(src, dst, sem, peer):
        copy = pltpu.make_async_remote_copy(
            src_ref=src, dst_ref=dst, send_sem=ss.at[sem], recv_sem=rs.at[sem],
            device_id=peer, device_id_type=MESH)
        copy.start()
        sent.append(copy)

    def arrived(dst, sem):
        pltpu.make_async_copy(dst, dst, rs.at[sem]).wait()

    def lanes(g):
        return pl.ds(pl.multiple_of(g * PAIR, PAIR), PAIR)

    def heads_of(dx, dc):
        return lanes(lax.rem(core + dc, 2) * NX + lax.rem(x + dx, NX))

    def x_back(dx):
        return lax.rem(x + NX - dx, NX)

    edge_row = 1 + 3 * core
    inner_row = 2 + core
    both_rows = pl.ds(2 * core, 2)
    quarter = pl.ds(pl.multiple_of(y * 32, 32), 32)
    half = pl.ds(pl.multiple_of(core * 1024, 1024), 1024)
    mine = heads_of(0, 0)

    keep(flags_hbm, flags, FLAGS)
    keep(k_hbm.at[core, 0, :, mine], kb.at[edge_row, 1 + x], KE)
    keep(v_hbm.at[core, 0, :, mine], vb.at[edge_row, 1 + x], VE)
    keep(ck_hbm.at[quarter, half], zk.at[zl], CZK)
    keep(cv_hbm.at[quarter, half], zv.at[zl], CZV)
    keep(q_hbm.at[:, 0, :, mine], qb.at[both_rows, x], QQ)
    keep(k_hbm.at[1 - core, 0, :, mine], kb.at[inner_row, 1 + x], KI)
    keep(v_hbm.at[1 - core, 0, :, mine], vb.at[inner_row, 1 + x], VI)

    bias[...] = jnp.zeros(bias.shape, jnp.float32)
    arrived(flags, FLAGS)
    for t in range(2):
        kept = flags[t]
        for a in range(3):
            for b in range(3):
                cell = (slice(a, a + 1), slice(b * 128, (b + 1) * 128))
                if a == 1 and b == 1:
                    continue
                grid_row = row * 2 + t + a - 1
                grid_col = col + b - 1
                inside = ((grid_row >= 0) & (grid_row < 2 * 2 * NP)
                          & (grid_col >= 0) & (grid_col < ZL * NX))
                flag = jnp.broadcast_to(kept[:, 3 * a + b:3 * a + b + 1], (1, 128))
                usable = (flag > 0) & jnp.broadcast_to(inside, (1, 128))
                bias[(t, *cell)] = jnp.where(usable, 0.0, -jnp.inf).astype(jnp.float32)
    keep(bias, bb.at[both_rows, x], BB)

    pl.semaphore_wait(barrier, len(callers))

    for src, buf, sem, far in ((ck_hbm, zk, CZK, 2), (cv_hbm, zv, CZV, -2)):
        send(src.at[quarter, half], buf.at[zl], sem + 1, along_z(1))
        send(src.at[quarter, half], buf.at[zl], sem + 3, along_z(-1))
        send(src.at[quarter, half], buf.at[zl], sem + 2, along_z(far))
    for dx, dc in mates:
        for src, buf, sem in ((k_hbm, kb, KE), (v_hbm, vb, VE)):
            send(src.at[core, 0, :, heads_of(dx, dc)], buf.at[edge_row, 1 + x], sem + dx * 2 + dc, along_x(dx, dc))

    def forward_rows(dx):
        j = x_back(dx)
        first, last = (3 - j) // 3, j // 3
        dst_col = 1 + j + 4 * first - 4 * last
        slot = j + 4 * first + 2 * last
        for top in (0, 1):
            dc = lax.rem(core + top, 2)
            src_row, dst_row, dp = ((1, 5, -1), (4, 0, 1))[top]
            for buf, esem, sem in ((kb, KE, RK), (vb, VE, RV)):
                arrived(buf.at[src_row, 1 + j], esem + dx * 2 + dc)
                send(buf.at[src_row, 1 + j], buf.at[dst_row, dst_col], sem + top * 6 + slot,
                     halo_target(dp, last - first))

    forward_rows(0)
    for buf, sem in ((zk, CZK), (zv, CZV)):
        for dz in range(ZL):
            arrived(buf.at[lax.rem(zl + ZL - dz, ZL)], sem + dz)
    for zbuf, buf, sem in ((zk, ckb, CXK), (zv, cvb, CXV)):
        for dx in (1, 3, 2):
            send(zbuf.at[:, :, lanes(lax.rem(x + dx, NX))], buf.at[y, :, x], sem + dx, along_x(dx, 0))
        keep(zbuf.at[:, :, lanes(x)], buf.at[y, :, x], sem)
    forward_rows(1)
    forward_rows(3)
    for dx, dc in mates:
        send(q_hbm.at[:, 0, :, heads_of(dx, dc)], qb.at[both_rows, x], QQ + dx * 2 + dc, along_x(dx, dc))
    forward_rows(2)
    for dx, dc in mates:
        send(bias, bb.at[both_rows, x], BB + dx * 2 + dc, along_x(dx, dc))
        for src, buf, sem in ((k_hbm, kb, KI), (v_hbm, vb, VI)):
            send(src.at[1 - core, 0, :, heads_of(dx, dc)], buf.at[inner_row, 1 + x], sem + dx * 2 + dc, along_x(dx, dc))

    for buf, xsem, ysem in ((ckb, CXK, CYK), (cvb, CXV, CYV)):
        for dx in range(NX):
            arrived(buf.at[y, :, x_back(dx)], xsem + dx)
        for dy in (1, 3, 2):
            send(buf.at[y], buf.at[y], ysem + dy, along_y(dy))

    factor = LOG2E * HEAD_DIM ** -0.5
    contract = (((1,), (1,)), ((), ()))

    def scored(i, j, h, near, coarse):
        heads = slice(h * HEAD_DIM, (h + 1) * HEAD_DIM)
        query = qb[i, j, :, heads]
        scores, values = [], []
        for a in near:
            keys = kb[i + a, pl.ds(j, 3), :, heads].reshape(3 * 128, HEAD_DIM)
            s = lax.dot_general(query, keys, contract, preferred_element_type=jnp.float32)
            scores.append(s + bb[i, j, a:a + 1, :])
            values.append(vb[i + a, pl.ds(j, 3), :, heads].reshape(3 * 128, HEAD_DIM))
        for dy in coarse:
            q_at = lax.rem(y + NY - dy, NY)
            keys = ckb[q_at, :, :, :, heads].reshape(512, HEAD_DIM)
            scores.append(lax.dot_general(query, keys, contract, preferred_element_type=jnp.float32))
            values.append(cvb[q_at, :, :, :, heads].reshape(512, HEAD_DIM))
        return scores, values

    def unit(i, j, near, coarse, start, finish):
        for h in (0, 1):
            scores, values = scored(i, j, h, near, coarse)
            slot = i * 4 + j
            largest = scores[0].max(-1, keepdims=True)
            for s in scores[1:]:
                largest = jnp.maximum(largest, s.max(-1, keepdims=True))
            if not start:
                before = mst[h, slot]
                largest = jnp.maximum(largest, before[:, :1])
            shift = largest * factor
            total, mixed = None, None
            for s, v in zip(scores, values):
                p = jnp.exp2(s * factor - shift)
                t = p.sum(-1, keepdims=True)
                o = jnp.dot(p.astype(jnp.bfloat16), v, preferred_element_type=jnp.float32)
                total = t if total is None else total + t
                mixed = o if mixed is None else mixed + o
            if not start:
                scale = jnp.exp2((before - largest) * factor)
                mixed = mixed + acc[h, slot] * scale
                total = total + lst[h, slot] * scale
            if finish:
                ob[i, j, :, h * HEAD_DIM:(h + 1) * HEAD_DIM] = (mixed / total).astype(jnp.bfloat16)
            else:
                acc[h, slot] = mixed
                mst[h, slot] = jnp.broadcast_to(largest, (128, 128))
                lst[h, slot] = jnp.broadcast_to(total, (128, 128))

    def give_back(out_sem, source_row, tile_of):
        for dx in (1, 3, 2, 0):
            for dc in (1, 0):
                to_x = lax.rem(x + dx, NX)
                to_c = lax.rem(core + dc, 2)
                src = ob.at[source_row(to_c), to_x]
                dst = out_hbm.at[tile_of(to_c), 0, :, mine]
                if dx or dc:
                    send(src, dst, out_sem + dx * 2 + dc, along_x(dx, dc))
                else:
                    keep(src, dst, out_sem)

    def get_back(out_sem, tile):
        for dx in range(NX):
            for dc in (0, 1):
                g = lax.rem(core + dc, 2) * NX + x_back(dx)
                arrived(out_hbm.at[tile, 0, :, lanes(g)], out_sem + dx * 2 + dc)

    for dx in range(NX):
        for dc in (0, 1):
            rows = pl.ds(2 * lax.rem(core + dc, 2), 2)
            arrived(qb.at[rows, x_back(dx)], QQ + dx * 2 + dc)
    for buf, ysem in ((ckb, CYK), (cvb, CYV)):
        arrived(buf.at[lax.rem(y + NY - 1, NY)], ysem + 1)

    @pl.loop(0, 16)
    def _(t):
        unit(t // 4, lax.rem(t, 4), (), (0, 1), True, False)

    for dx in range(NX):
        j = x_back(dx)
        for s in (0, 1):
            dc = lax.rem(core + s, 2)
            arrived(kb.at[2 + s, 1 + j], KI + dx * 2 + dc)
            arrived(vb.at[2 + s, 1 + j], VI + dx * 2 + dc)
    for buf, sem in ((kb, HK), (vb, HV)):
        send(buf.at[pl.ds(1, 4), 4], buf.at[pl.ds(1, 4), 0], sem, along_z(1))
        send(buf.at[pl.ds(1, 4), 1], buf.at[pl.ds(1, 4), 5], sem + 1, along_z(-1))
    for top, r in ((0, 5), (1, 0)):
        for buf, sem in ((kb, RK), (vb, RV)):
            for slot, from_col, to_col, j, dz in ((4, 5, 1, 0, 1), (5, 0, 4, 3, -1)):
                arrived(buf.at[r, from_col], sem + top * 6 + slot)
                send(buf.at[r, from_col], buf.at[r, to_col], sem + top * 6 + j, along_z(dz))

    for buf, ysem in ((ckb, CYK), (cvb, CYV)):
        for dy in (3, 2):
            arrived(buf.at[lax.rem(y + NY - dy, NY)], ysem + dy)

    @pl.loop(0, 16)
    def _(t):
        unit(t // 4, lax.rem(t, 4), (), (2, 3), False, False)

    for dx in range(NX):
        for dc in (0, 1):
            rows = pl.ds(2 * lax.rem(core + dc, 2), 2)
            arrived(bb.at[rows, x_back(dx)], BB + dx * 2 + dc)
    for buf, sem in ((kb, HK), (vb, HV)):
        arrived(buf.at[pl.ds(1, 4), 0], sem)
        arrived(buf.at[pl.ds(1, 4), 5], sem + 1)

    @pl.loop(0, 8)
    def _(t):
        unit(1 + t // 4, lax.rem(t, 4), (0, 1, 2), (), False, True)

    give_back(OI, lambda c: 1 + c, lambda c: 1 - c)

    for i, rows in ((0, (1, 2)), (3, (0, 1))):
        @pl.loop(0, 4)
        def _(j):
            unit(i, j, rows, (), False, False)

    for top, r, i, a in ((0, 5, 3, 2), (1, 0, 0, 0)):
        for buf, sem in ((kb, RK), (vb, RV)):
            for j in range(4):
                arrived(buf.at[r, 1 + j], sem + top * 6 + j)

    for i, a in ((0, 0), (3, 2)):
        @pl.loop(0, 4)
        def _(j):
            unit(i, j, (a,), (), False, True)

    give_back(OE, lambda c: 3 * c, lambda c: c)
    get_back(OI, 1 - core)
    get_back(OE, core)
    for copy in sent:
        copy.wait_send()


def body(queries, fine_keys, fine_values, keep_flags, coarse_keys, coarse_values):
    bf16, f32 = jnp.bfloat16, jnp.float32
    return pl.pallas_call(
        kernel,
        out_shape=jax.ShapeDtypeStruct(queries.shape, bf16),
        in_specs=[pl.BlockSpec(memory_space=pltpu.HBM)] * 6,
        out_specs=pl.BlockSpec(memory_space=pltpu.HBM),
        scratch_shapes=[
            pltpu.VMEM((4, 4, 128, PAIR), bf16),
            pltpu.VMEM((6, 6, 128, PAIR), bf16),
            pltpu.VMEM((6, 6, 128, PAIR), bf16),
            pltpu.VMEM((2, 1, 9), jnp.int32),
            pltpu.VMEM((2, 8, 384), f32),
            pltpu.VMEM((4, 4, 8, 384), f32),
            pltpu.VMEM((ZL, 32, 1024), bf16),
            pltpu.VMEM((ZL, 32, 1024), bf16),
            pltpu.VMEM((NY, ZL, NX, 32, PAIR), bf16),
            pltpu.VMEM((NY, ZL, NX, 32, PAIR), bf16),
            pltpu.VMEM((4, 4, 128, PAIR), bf16),
            pltpu.VMEM((2, 16, 128, 128), f32),
            pltpu.VMEM((2, 16, 128, 128), f32),
            pltpu.VMEM((2, 16, 128, 128), f32),
            pltpu.SemaphoreType.DMA((SEMS,)),
            pltpu.SemaphoreType.DMA((SEMS,)),
        ],
        compiler_params=pltpu.CompilerParams(
            collective_id=0, has_side_effects=True, vmem_limit_bytes=VMEM_LIMIT),
        name="window_attention",
    )(queries, fine_keys, fine_values, keep_flags, coarse_keys, coarse_values)


VMEM_LIMIT = 63 << 20


def solution(mesh):
    placed = (
        P("row", "col", None, None),
        P("row", "col", None, None),
        P("row", "col", None, None),
        P("row", "col", None),
        P("col", None),
        P("col", None),
    )
    return jax.shard_map(
        body, mesh=mesh, in_specs=placed, out_specs=P("row", "col", None, None), check_vma=False
    )
```

time: 143 us -> 128 us (0.90)
  the two profiles are of different devices: /device:TPU:1 before, /device:TPU:31 now
where the time goes in v2:
time: 128 us; the launch traced here: 127 us
  Pallas kernels  125 us (98%)
  local copies, waits for them, and re-layouts  2.3 us (2%)
    pallas_call x1, Pallas kernels, body(): pl.pallas_call(kernel, out_shape=jax.ShapeDtypeStruct(queries.shape, bf16...  125 us

profile of v2, /device:TPU:31, one launch (start us, length us, event | category | flops | bytes accessed | tf_op | source)
XLA Modules:
  0.0 127.1 jit_solution(12668767681042735793)
XLA Ops:
  0.0 124.8 %window_attention.1 = bf16[2,1,128,2048]{3,2,1,0:T(8,128)(2,1)} custom-call(bf16[2,1,128,2048]{3,2,1,0:T(8,128)(2,1)} %q_hbm.1, bf16[2,1,128,2048]{3,2,1,0:T(8,128)(2,1)} %k_hbm.1, bf16[2,1,128,2048]{3,2,1,0:T(8,128)(2,1)} %v_hbm.1, s32[2,1,9]{2,1,0:T(1,128)} %flags_hbm.1, bf16[128,2048]{1,0:T(8,128)(2,1)} %ck_hbm.1, bf16[128,2048]{1,0:T(8,128)(2,1)} %cv_hbm.1), custom_call_target="tpu_custom_call" | custom-call | tf_op jit(solution)/shard_map/window_attention/pallas_call | solution.py:313
  124.8 2.3 %copy.8 = bf16[2,1,128,2048]{3,2,1,0:T(8,128)(2,1)} copy(bf16[2,1,128,2048]{3,2,1,0:T(8,128)(2,1)} %window_attention.1) | data formatting | bytes 2097152

commit v3 on v2

--- a/solution.py
+++ b/solution.py
@@ -175,46 +175,51 @@
     factor = LOG2E * HEAD_DIM ** -0.5
     contract = (((1,), (1,)), ((), ()))
 
-    def scored(i, j, h, near, coarse):
-        heads = slice(h * HEAD_DIM, (h + 1) * HEAD_DIM)
-        query = qb[i, j, :, heads]
-        scores, values = [], []
-        for a in near:
-            keys = kb[i + a, pl.ds(j, 3), :, heads].reshape(3 * 128, HEAD_DIM)
-            s = lax.dot_general(query, keys, contract, preferred_element_type=jnp.float32)
-            scores.append(s + bb[i, j, a:a + 1, :])
-            values.append(vb[i + a, pl.ds(j, 3), :, heads].reshape(3 * 128, HEAD_DIM))
-        for dy in coarse:
-            q_at = lax.rem(y + NY - dy, NY)
-            keys = ckb[q_at, :, :, :, heads].reshape(512, HEAD_DIM)
-            scores.append(lax.dot_general(query, keys, contract, preferred_element_type=jnp.float32))
-            values.append(cvb[q_at, :, :, :, heads].reshape(512, HEAD_DIM))
-        return scores, values
-
-    def unit(i, j, near, coarse, start, finish):
-        for h in (0, 1):
-            scores, values = scored(i, j, h, near, coarse)
-            slot = i * 4 + j
+    def units(i, near, coarse, start, finish):
+        chains = [(j, h, slice(h * HEAD_DIM, (h + 1) * HEAD_DIM)) for j in range(4) for h in (0, 1)]
+        scored = []
+        for j, h, heads in chains:
+            query = qb[i, j, :, heads]
+            scores = []
+            for a in near:
+                keys = kb[i + a, j:j + 3, :, heads].reshape(3 * 128, HEAD_DIM)
+                s = lax.dot_general(query, keys, contract, preferred_element_type=jnp.float32)
+                scores.append(s + bb[i, j, a:a + 1, :])
+            for dy in coarse:
+                keys = ckb[lax.rem(y + NY - dy, NY), :, :, :, heads].reshape(512, HEAD_DIM)
+                scores.append(lax.dot_general(query, keys, contract, preferred_element_type=jnp.float32))
             largest = scores[0].max(-1, keepdims=True)
             for s in scores[1:]:
                 largest = jnp.maximum(largest, s.max(-1, keepdims=True))
+            before = None
             if not start:
-                before = mst[h, slot]
+                before = mst[h, i * 4 + j]
                 largest = jnp.maximum(largest, before[:, :1])
+            scored.append((scores, largest, before))
+        weighed = []
+        for scores, largest, before in scored:
             shift = largest * factor
-            total, mixed = None, None
-            for s, v in zip(scores, values):
+            total, probs = None, []
+            for s in scores:
                 p = jnp.exp2(s * factor - shift)
                 t = p.sum(-1, keepdims=True)
-                o = jnp.dot(p.astype(jnp.bfloat16), v, preferred_element_type=jnp.float32)
                 total = t if total is None else total + t
+                probs.append(p.astype(jnp.bfloat16))
+            weighed.append((probs, total))
+        for (j, h, heads), (scores, largest, before), (probs, total) in zip(chains, scored, weighed):
+            slot = i * 4 + j
+            values = [vb[i + a, j:j + 3, :, heads].reshape(3 * 128, HEAD_DIM) for a in near]
+            values += [cvb[lax.rem(y + NY - dy, NY), :, :, :, heads].reshape(512, HEAD_DIM) for dy in coarse]
+            mixed = None
+            for p, v in zip(probs, values):
+                o = jnp.dot(p, v, preferred_element_type=jnp.float32)
                 mixed = o if mixed is None else mixed + o
             if not start:
                 scale = jnp.exp2((before - largest) * factor)
                 mixed = mixed + acc[h, slot] * scale
                 total = total + lst[h, slot] * scale
             if finish:
-                ob[i, j, :, h * HEAD_DIM:(h + 1) * HEAD_DIM] = (mixed / total).astype(jnp.bfloat16)
+                ob[i, j, :, heads] = (mixed / total).astype(jnp.bfloat16)
             else:
                 acc[h, slot] = mixed
                 mst[h, slot] = jnp.broadcast_to(largest, (128, 128))
@@ -245,9 +250,9 @@
     for buf, ysem in ((ckb, CYK), (cvb, CYV)):
         arrived(buf.at[lax.rem(y + NY - 1, NY)], ysem + 1)
 
-    @pl.loop(0, 16)
-    def _(t):
-        unit(t // 4, lax.rem(t, 4), (), (0, 1), True, False)
+    @pl.loop(0, 4)
+    def _(i):
+        units(i, (), (0, 1), True, False)
 
     for dx in range(NX):
         j = x_back(dx)
@@ -268,9 +273,9 @@
         for dy in (3, 2):
             arrived(buf.at[lax.rem(y + NY - dy, NY)], ysem + dy)
 
-    @pl.loop(0, 16)
-    def _(t):
-        unit(t // 4, lax.rem(t, 4), (), (2, 3), False, False)
+    @pl.loop(0, 4)
+    def _(i):
+        units(i, (), (2, 3), False, False)
 
     for dx in range(NX):
         for dc in (0, 1):
@@ -280,26 +285,22 @@
         arrived(buf.at[pl.ds(1, 4), 0], sem)
         arrived(buf.at[pl.ds(1, 4), 5], sem + 1)
 
-    @pl.loop(0, 8)
-    def _(t):
-        unit(1 + t // 4, lax.rem(t, 4), (0, 1, 2), (), False, True)
+    @pl.loop(1, 3)
+    def _(i):
+        units(i, (0, 1, 2), (), False, True)
 
     give_back(OI, lambda c: 1 + c, lambda c: 1 - c)
 
-    for i, rows in ((0, (1, 2)), (3, (0, 1))):
-        @pl.loop(0, 4)
-        def _(j):
-            unit(i, j, rows, (), False, False)
-
-    for top, r, i, a in ((0, 5, 3, 2), (1, 0, 0, 0)):
+    units(0, (1, 2), (), False, False)
+    units(3, (0, 1), (), False, False)
+
+    for top, r in ((1, 0), (0, 5)):
         for buf, sem in ((kb, RK), (vb, RV)):
             for j in range(4):
                 arrived(buf.at[r, 1 + j], sem + top * 6 + j)
 
-    for i, a in ((0, 0), (3, 2)):
-        @pl.loop(0, 4)
-        def _(j):
-            unit(i, j, (a,), (), False, True)
+    units(0, (0,), (), False, True)
+    units(3, (2,), (), False, True)
 
     give_back(OE, lambda c: 3 * c, lambda c: c)
     get_back(OI, 1 - core)

time: 128 us -> 108 us (0.84)
  Pallas kernels: 125 us -> 105 us
    pallas_call x1, Pallas kernels: 125 us -> 105 us  [body(): pl.pallas_call(kernel, out_shape=jax.ShapeDtypeStruct(queries.shape, bf16...]
where the time goes in v3:
time: 108 us; the launch traced here: 107 us
  Pallas kernels  105 us (97%)
  local copies, waits for them, and re-layouts  2.3 us (2%)
    pallas_call x1, Pallas kernels, body(): pl.pallas_call(kernel, out_shape=jax.ShapeDtypeStruct(queries.shape, bf16...  105 us
    unnamed x1, local copies, waits for them, and re-layouts  2.3 us

profile of v3, /device:TPU:31, one launch (start us, length us, event | category | flops | bytes accessed | tf_op | source)
XLA Modules:
  0.0 106.9 jit_solution(14781885829001015669)
XLA Ops:
  0.0 104.6 %window_attention.1 = bf16[2,1,128,2048]{3,2,1,0:T(8,128)(2,1)} custom-call(bf16[2,1,128,2048]{3,2,1,0:T(8,128)(2,1)} %q_hbm.1, bf16[2,1,128,2048]{3,2,1,0:T(8,128)(2,1)} %k_hbm.1, bf16[2,1,128,2048]{3,2,1,0:T(8,128)(2,1)} %v_hbm.1, s32[2,1,9]{2,1,0:T(1,128)} %flags_hbm.1, bf16[128,2048]{1,0:T(8,128)(2,1)} %ck_hbm.1, bf16[128,2048]{1,0:T(8,128)(2,1)} %cv_hbm.1), custom_call_target="tpu_custom_call" | custom-call | tf_op jit(solution)/shard_map/window_attention/pallas_call | solution.py:314
  104.6 2.3 %copy.8 = bf16[2,1,128,2048]{3,2,1,0:T(8,128)(2,1)} copy(bf16[2,1,128,2048]{3,2,1,0:T(8,128)(2,1)} %window_attention.1) | data formatting | bytes 2097152

commit v4 on v3

--- a/solution.py
+++ b/solution.py
@@ -159,18 +159,28 @@
     forward_rows(1)
     forward_rows(3)
     for dx, dc in mates:
-        send(q_hbm.at[:, 0, :, heads_of(dx, dc)], qb.at[both_rows, x], QQ + dx * 2 + dc, along_x(dx, dc))
+        for src, buf, sem in ((k_hbm, kb, KI), (v_hbm, vb, VI)):
+            send(src.at[1 - core, 0, :, heads_of(dx, dc)], buf.at[inner_row, 1 + x], sem + dx * 2 + dc, along_x(dx, dc))
     forward_rows(2)
     for dx, dc in mates:
+        send(q_hbm.at[:, 0, :, heads_of(dx, dc)], qb.at[both_rows, x], QQ + dx * 2 + dc, along_x(dx, dc))
         send(bias, bb.at[both_rows, x], BB + dx * 2 + dc, along_x(dx, dc))
-        for src, buf, sem in ((k_hbm, kb, KI), (v_hbm, vb, VI)):
-            send(src.at[1 - core, 0, :, heads_of(dx, dc)], buf.at[inner_row, 1 + x], sem + dx * 2 + dc, along_x(dx, dc))
 
     for buf, xsem, ysem in ((ckb, CXK, CYK), (cvb, CXV, CYV)):
         for dx in range(NX):
             arrived(buf.at[y, :, x_back(dx)], xsem + dx)
         for dy in (1, 3, 2):
             send(buf.at[y], buf.at[y], ysem + dy, along_y(dy))
+
+    for dx in range(NX):
+        j = x_back(dx)
+        for s in (0, 1):
+            dc = lax.rem(core + s, 2)
+            arrived(kb.at[2 + s, 1 + j], KI + dx * 2 + dc)
+            arrived(vb.at[2 + s, 1 + j], VI + dx * 2 + dc)
+    for buf, sem in ((kb, HK), (vb, HV)):
+        send(buf.at[pl.ds(1, 4), 4], buf.at[pl.ds(1, 4), 0], sem, along_z(1))
+        send(buf.at[pl.ds(1, 4), 1], buf.at[pl.ds(1, 4), 5], sem + 1, along_z(-1))
 
     factor = LOG2E * HEAD_DIM ** -0.5
     contract = (((1,), (1,)), ((), ()))
@@ -184,7 +194,7 @@
             for a in near:
                 keys = kb[i + a, j:j + 3, :, heads].reshape(3 * 128, HEAD_DIM)
                 s = lax.dot_general(query, keys, contract, preferred_element_type=jnp.float32)
-                scores.append(s + bb[i, j, a:a + 1, :])
+                scores.append(s + bb[i, j, pl.ds(a, 1), :])
             for dy in coarse:
                 keys = ckb[lax.rem(y + NY - dy, NY), :, :, :, heads].reshape(512, HEAD_DIM)
                 scores.append(lax.dot_general(query, keys, contract, preferred_element_type=jnp.float32))
@@ -254,15 +264,6 @@
     def _(i):
         units(i, (), (0, 1), True, False)
 
-    for dx in range(NX):
-        j = x_back(dx)
-        for s in (0, 1):
-            dc = lax.rem(core + s, 2)
-            arrived(kb.at[2 + s, 1 + j], KI + dx * 2 + dc)
-            arrived(vb.at[2 + s, 1 + j], VI + dx * 2 + dc)
-    for buf, sem in ((kb, HK), (vb, HV)):
-        send(buf.at[pl.ds(1, 4), 4], buf.at[pl.ds(1, 4), 0], sem, along_z(1))
-        send(buf.at[pl.ds(1, 4), 1], buf.at[pl.ds(1, 4), 5], sem + 1, along_z(-1))
     for top, r in ((0, 5), (1, 0)):
         for buf, sem in ((kb, RK), (vb, RV)):
             for slot, from_col, to_col, j, dz in ((4, 5, 1, 0, 1), (5, 0, 4, 3, -1)):
@@ -291,20 +292,36 @@
 
     give_back(OI, lambda c: 1 + c, lambda c: 1 - c)
 
-    units(0, (1, 2), (), False, False)
-    units(3, (0, 1), (), False, False)
+    @pl.loop(0, 2)
+    def _(u):
+        units(3 * u, (1 - u, 2 - u), (), False, False)
 
     for top, r in ((1, 0), (0, 5)):
         for buf, sem in ((kb, RK), (vb, RV)):
             for j in range(4):
                 arrived(buf.at[r, 1 + j], sem + top * 6 + j)
 
-    units(0, (0,), (), False, True)
-    units(3, (2,), (), False, True)
-
-    give_back(OE, lambda c: 3 * c, lambda c: c)
+    def outer_back(u, dx):
+        to_x = lax.rem(x + dx, NX)
+        sem = OE + dx * 2 + lax.rem(core + u, 2)
+        return pltpu.make_async_remote_copy(
+            src_ref=ob.at[3 * u, to_x], dst_ref=out_hbm.at[u, 0, :, mine],
+            send_sem=ss.at[sem], recv_sem=rs.at[sem],
+            device_id=at(to_x, y, z, u), device_id_type=MESH)
+
+    @pl.loop(0, 2)
+    def _(u):
+        units(3 * u, (2 * u,), (), False, True)
+        for dx in (1, 3, 2):
+            outer_back(u, dx).start()
+
+    send(ob.at[3 * (1 - core), x], out_hbm.at[1 - core, 0, :, mine], OE + 1, along_x(0, 1))
+    keep(ob.at[3 * core, x], out_hbm.at[core, 0, :, mine], OE)
     get_back(OI, 1 - core)
     get_back(OE, core)
+    for u in (0, 1):
+        for dx in (1, 2, 3):
+            outer_back(u, dx).wait_send()
     for copy in sent:
         copy.wait_send()
 

time: 108 us -> 107 us (level)
  no operation moved by 1% of the time
where the time goes in v4:
time: 107 us
  Pallas kernels  105 us (98%)
  local copies, waits for them, and re-layouts  2.3 us (2%)
    pallas_call x1, Pallas kernels, body(): pl.pallas_call(kernel, out_shape=jax.ShapeDtypeStruct(queries.shape, bf16...  105 us
    unnamed x1, local copies, waits for them, and re-layouts  2.3 us

profile of v4, /device:TPU:31, one launch (start us, length us, event | category | flops | bytes accessed | tf_op | source)
XLA Modules:
  0.0 106.9 jit_solution(9077315907664773581)
XLA Ops:
  0.0 104.6 %window_attention.1 = bf16[2,1,128,2048]{3,2,1,0:T(8,128)(2,1)} custom-call(bf16[2,1,128,2048]{3,2,1,0:T(8,128)(2,1)} %q_hbm.1, bf16[2,1,128,2048]{3,2,1,0:T(8,128)(2,1)} %k_hbm.1, bf16[2,1,128,2048]{3,2,1,0:T(8,128)(2,1)} %v_hbm.1, s32[2,1,9]{2,1,0:T(1,128)} %flags_hbm.1, bf16[128,2048]{1,0:T(8,128)(2,1)} %ck_hbm.1, bf16[128,2048]{1,0:T(8,128)(2,1)} %cv_hbm.1), custom_call_target="tpu_custom_call" | custom-call | tf_op jit(solution)/shard_map/window_attention/pallas_call | solution.py:331
  104.6 2.3 %copy.8 = bf16[2,1,128,2048]{3,2,1,0:T(8,128)(2,1)} copy(bf16[2,1,128,2048]{3,2,1,0:T(8,128)(2,1)} %window_attention.1) | data formatting | bytes 2097152

commit v5 on v4

--- a/solution.py
+++ b/solution.py
@@ -135,20 +135,16 @@
         for src, buf, sem in ((k_hbm, kb, KE), (v_hbm, vb, VE)):
             send(src.at[core, 0, :, heads_of(dx, dc)], buf.at[edge_row, 1 + x], sem + dx * 2 + dc, along_x(dx, dc))
 
-    def forward_rows(dx):
-        j = x_back(dx)
-        first, last = (3 - j) // 3, j // 3
-        dst_col = 1 + j + 4 * first - 4 * last
-        slot = j + 4 * first + 2 * last
+    def forward_rows(j):
+        dst_col, slot, dz = {0: (5, 4, -1), 1: (2, 1, 0), 2: (3, 2, 0), 3: (0, 5, 1)}[j]
+        dx = lax.rem(x + NX - j, NX)
         for top in (0, 1):
             dc = lax.rem(core + top, 2)
             src_row, dst_row, dp = ((1, 5, -1), (4, 0, 1))[top]
             for buf, esem, sem in ((kb, KE, RK), (vb, VE, RV)):
                 arrived(buf.at[src_row, 1 + j], esem + dx * 2 + dc)
-                send(buf.at[src_row, 1 + j], buf.at[dst_row, dst_col], sem + top * 6 + slot,
-                     halo_target(dp, last - first))
-
-    forward_rows(0)
+                send(buf.at[src_row, 1 + j], buf.at[dst_row, dst_col], sem + top * 6 + slot, halo_target(dp, dz))
+
     for buf, sem in ((zk, CZK), (zv, CZV)):
         for dz in range(ZL):
             arrived(buf.at[lax.rem(zl + ZL - dz, ZL)], sem + dz)
@@ -156,12 +152,11 @@
         for dx in (1, 3, 2):
             send(zbuf.at[:, :, lanes(lax.rem(x + dx, NX))], buf.at[y, :, x], sem + dx, along_x(dx, 0))
         keep(zbuf.at[:, :, lanes(x)], buf.at[y, :, x], sem)
-    forward_rows(1)
-    forward_rows(3)
     for dx, dc in mates:
         for src, buf, sem in ((k_hbm, kb, KI), (v_hbm, vb, VI)):
             send(src.at[1 - core, 0, :, heads_of(dx, dc)], buf.at[inner_row, 1 + x], sem + dx * 2 + dc, along_x(dx, dc))
-    forward_rows(2)
+    forward_rows(0)
+    forward_rows(3)
     for dx, dc in mates:
         send(q_hbm.at[:, 0, :, heads_of(dx, dc)], qb.at[both_rows, x], QQ + dx * 2 + dc, along_x(dx, dc))
         send(bias, bb.at[both_rows, x], BB + dx * 2 + dc, along_x(dx, dc))
@@ -181,22 +176,24 @@
     for buf, sem in ((kb, HK), (vb, HV)):
         send(buf.at[pl.ds(1, 4), 4], buf.at[pl.ds(1, 4), 0], sem, along_z(1))
         send(buf.at[pl.ds(1, 4), 1], buf.at[pl.ds(1, 4), 5], sem + 1, along_z(-1))
+    forward_rows(1)
+    forward_rows(2)
 
     factor = LOG2E * HEAD_DIM ** -0.5
     contract = (((1,), (1,)), ((), ()))
 
-    def units(i, near, coarse, start, finish):
-        chains = [(j, h, slice(h * HEAD_DIM, (h + 1) * HEAD_DIM)) for j in range(4) for h in (0, 1)]
-        scored = []
-        for j, h, heads in chains:
+    def units(i, tiles, near, coarse, start, finish):
+        chains = [(j, slice(h * HEAD_DIM, (h + 1) * HEAD_DIM), h) for j in tiles for h in (0, 1)]
+
+        def scores_of(j, heads, h):
             query = qb[i, j, :, heads]
             scores = []
             for a in near:
                 keys = kb[i + a, j:j + 3, :, heads].reshape(3 * 128, HEAD_DIM)
                 s = lax.dot_general(query, keys, contract, preferred_element_type=jnp.float32)
                 scores.append(s + bb[i, j, pl.ds(a, 1), :])
-            for dy in coarse:
-                keys = ckb[lax.rem(y + NY - dy, NY), :, :, :, heads].reshape(512, HEAD_DIM)
+            for part in coarse:
+                keys = ckb[part, :, :, :, heads].reshape(512, HEAD_DIM)
                 scores.append(lax.dot_general(query, keys, contract, preferred_element_type=jnp.float32))
             largest = scores[0].max(-1, keepdims=True)
             for s in scores[1:]:
@@ -205,9 +202,9 @@
             if not start:
                 before = mst[h, i * 4 + j]
                 largest = jnp.maximum(largest, before[:, :1])
-            scored.append((scores, largest, before))
-        weighed = []
-        for scores, largest, before in scored:
+            return scores, largest, before
+
+        def probs_of(scores, largest, before):
             shift = largest * factor
             total, probs = None, []
             for s in scores:
@@ -215,11 +212,12 @@
                 t = p.sum(-1, keepdims=True)
                 total = t if total is None else total + t
                 probs.append(p.astype(jnp.bfloat16))
-            weighed.append((probs, total))
-        for (j, h, heads), (scores, largest, before), (probs, total) in zip(chains, scored, weighed):
+            return probs, total
+
+        def mix(j, heads, h, largest, before, probs, total):
             slot = i * 4 + j
             values = [vb[i + a, j:j + 3, :, heads].reshape(3 * 128, HEAD_DIM) for a in near]
-            values += [cvb[lax.rem(y + NY - dy, NY), :, :, :, heads].reshape(512, HEAD_DIM) for dy in coarse]
+            values += [cvb[part, :, :, :, heads].reshape(512, HEAD_DIM) for part in coarse]
             mixed = None
             for p, v in zip(probs, values):
                 o = jnp.dot(p, v, preferred_element_type=jnp.float32)
@@ -235,6 +233,20 @@
                 mst[h, slot] = jnp.broadcast_to(largest, (128, 128))
                 lst[h, slot] = jnp.broadcast_to(total, (128, 128))
 
+        if coarse:
+            held = None
+            for chain in chains + [None]:
+                ahead = None if chain is None else (chain, scores_of(*chain))
+                if held is not None:
+                    (chain_, scored) = held
+                    mix(*chain_, *scored[1:], *probs_of(*scored))
+                held = ahead
+        else:
+            scored = [scores_of(*chain) for chain in chains]
+            weighed = [probs_of(*sc) for sc in scored]
+            for chain, sc, w in zip(chains, scored, weighed):
+                mix(*chain, *sc[1:], *w)
+
     def give_back(out_sem, source_row, tile_of):
         for dx in (1, 3, 2, 0):
             for dc in (1, 0):
@@ -257,12 +269,22 @@
         for dc in (0, 1):
             rows = pl.ds(2 * lax.rem(core + dc, 2), 2)
             arrived(qb.at[rows, x_back(dx)], QQ + dx * 2 + dc)
+            arrived(bb.at[rows, x_back(dx)], BB + dx * 2 + dc)
     for buf, ysem in ((ckb, CYK), (cvb, CYV)):
-        arrived(buf.at[lax.rem(y + NY - 1, NY)], ysem + 1)
-
-    @pl.loop(0, 4)
-    def _(i):
-        units(i, (), (0, 1), True, False)
+        for dy in (1, 3, 2):
+            arrived(buf.at[lax.rem(y + NY - dy, NY)], ysem + dy)
+    def inner_rows(tiles):
+        @pl.loop(1, 3)
+        def _(i):
+            units(i, tiles, (0, 1, 2), range(NY), True, True)
+
+    def outer_rows(tiles):
+        @pl.loop(0, 2)
+        def _(u):
+            units(3 * u, tiles, (1 - u, 2 - u), range(NY), True, False)
+
+    inner_rows((1, 2))
+    outer_rows((1, 2))
 
     for top, r in ((0, 5), (1, 0)):
         for buf, sem in ((kb, RK), (vb, RV)):
@@ -270,31 +292,12 @@
                 arrived(buf.at[r, from_col], sem + top * 6 + slot)
                 send(buf.at[r, from_col], buf.at[r, to_col], sem + top * 6 + j, along_z(dz))
 
-    for buf, ysem in ((ckb, CYK), (cvb, CYV)):
-        for dy in (3, 2):
-            arrived(buf.at[lax.rem(y + NY - dy, NY)], ysem + dy)
-
-    @pl.loop(0, 4)
-    def _(i):
-        units(i, (), (2, 3), False, False)
-
-    for dx in range(NX):
-        for dc in (0, 1):
-            rows = pl.ds(2 * lax.rem(core + dc, 2), 2)
-            arrived(bb.at[rows, x_back(dx)], BB + dx * 2 + dc)
     for buf, sem in ((kb, HK), (vb, HV)):
         arrived(buf.at[pl.ds(1, 4), 0], sem)
         arrived(buf.at[pl.ds(1, 4), 5], sem + 1)
-
-    @pl.loop(1, 3)
-    def _(i):
-        units(i, (0, 1, 2), (), False, True)
-
+    inner_rows((0, 3))
     give_back(OI, lambda c: 1 + c, lambda c: 1 - c)
-
-    @pl.loop(0, 2)
-    def _(u):
-        units(3 * u, (1 - u, 2 - u), (), False, False)
+    outer_rows((0, 3))
 
     for top, r in ((1, 0), (0, 5)):
         for buf, sem in ((kb, RK), (vb, RV)):
@@ -311,7 +314,7 @@
 
     @pl.loop(0, 2)
     def _(u):
-        units(3 * u, (2 * u,), (), False, True)
+        units(3 * u, range(4), (2 * u,), (), False, True)
         for dx in (1, 3, 2):
             outer_back(u, dx).start()
 

time: 107 us -> 96.8 us (0.905)
  the two profiles are of different devices: /device:TPU:31 before, /device:TPU:1 now
where the time goes in v5:
time: 96.8 us; the launch traced here: 96.7 us
  Pallas kernels  94.4 us (98%)
  local copies, waits for them, and re-layouts  2.3 us (2%)
    pallas_call x1, Pallas kernels, body(): pl.pallas_call(kernel, out_shape=jax.ShapeDtypeStruct(queries.shape, bf16...  94.4 us
    unnamed x1, local copies, waits for them, and re-layouts  2.3 us

profile of v5, /device:TPU:1, one launch (start us, length us, event | category | flops | bytes accessed | tf_op | source)
XLA Modules:
  0.0 96.7 jit_solution(1528908875087329793)
XLA Ops:
  0.0 94.4 %window_attention.1 = bf16[2,1,128,2048]{3,2,1,0:T(8,128)(2,1)} custom-call(bf16[2,1,128,2048]{3,2,1,0:T(8,128)(2,1)} %q_hbm.1, bf16[2,1,128,2048]{3,2,1,0:T(8,128)(2,1)} %k_hbm.1, bf16[2,1,128,2048]{3,2,1,0:T(8,128)(2,1)} %v_hbm.1, s32[2,1,9]{2,1,0:T(1,128)} %flags_hbm.1, bf16[128,2048]{1,0:T(8,128)(2,1)} %ck_hbm.1, bf16[128,2048]{1,0:T(8,128)(2,1)} %cv_hbm.1), custom_call_target="tpu_custom_call" | custom-call | tf_op jit(solution)/shard_map/window_attention/pallas_call | solution.py:334
  94.4 2.3 %copy.8 = bf16[2,1,128,2048]{3,2,1,0:T(8,128)(2,1)} copy(bf16[2,1,128,2048]{3,2,1,0:T(8,128)(2,1)} %window_attention.1) | data formatting | bytes 2097152

commit v6 on v5

--- a/solution.py
+++ b/solution.py
@@ -167,17 +167,22 @@
         for dy in (1, 3, 2):
             send(buf.at[y], buf.at[y], ysem + dy, along_y(dy))
 
-    for dx in range(NX):
-        j = x_back(dx)
+    def inner_tiles(j):
+        dx = lax.rem(x + NX - j, NX)
         for s in (0, 1):
             dc = lax.rem(core + s, 2)
             arrived(kb.at[2 + s, 1 + j], KI + dx * 2 + dc)
             arrived(vb.at[2 + s, 1 + j], VI + dx * 2 + dc)
+
+    inner_tiles(0)
+    inner_tiles(3)
     for buf, sem in ((kb, HK), (vb, HV)):
         send(buf.at[pl.ds(1, 4), 4], buf.at[pl.ds(1, 4), 0], sem, along_z(1))
         send(buf.at[pl.ds(1, 4), 1], buf.at[pl.ds(1, 4), 5], sem + 1, along_z(-1))
     forward_rows(1)
     forward_rows(2)
+    inner_tiles(1)
+    inner_tiles(2)
 
     factor = LOG2E * HEAD_DIM ** -0.5
     contract = (((1,), (1,)), ((), ()))
@@ -299,10 +304,6 @@
     give_back(OI, lambda c: 1 + c, lambda c: 1 - c)
     outer_rows((0, 3))
 
-    for top, r in ((1, 0), (0, 5)):
-        for buf, sem in ((kb, RK), (vb, RV)):
-            for j in range(4):
-                arrived(buf.at[r, 1 + j], sem + top * 6 + j)
 
     def outer_back(u, dx):
         to_x = lax.rem(x + dx, NX)
@@ -314,6 +315,9 @@
 
     @pl.loop(0, 2)
     def _(u):
+        for buf, sem in ((kb, RK), (vb, RV)):
+            for j in range(4):
+                arrived(buf.at[5 * u, 1 + j], sem + (1 - u) * 6 + j)
         units(3 * u, range(4), (2 * u,), (), False, True)
         for dx in (1, 3, 2):
             outer_back(u, dx).start()

time: 96.8 us -> 96.7 us (level)
  no operation moved by 1% of the time
where the time goes in v6:
time: 96.7 us; the launch traced here: 96.6 us
  Pallas kernels  94.3 us (98%)
  local copies, waits for them, and re-layouts  2.3 us (2%)
    pallas_call x1, Pallas kernels, body(): pl.pallas_call(kernel, out_shape=jax.ShapeDtypeStruct(queries.shape, bf16...  94.3 us
    unnamed x1, local copies, waits for them, and re-layouts  2.3 us

profile of v6, /device:TPU:1, one launch (start us, length us, event | category | flops | bytes accessed | tf_op | source)
XLA Modules:
  0.0 96.6 jit_solution(18226056856147668365)
XLA Ops:
  0.0 94.3 %window_attention.1 = bf16[2,1,128,2048]{3,2,1,0:T(8,128)(2,1)} custom-call(bf16[2,1,128,2048]{3,2,1,0:T(8,128)(2,1)} %q_hbm.1, bf16[2,1,128,2048]{3,2,1,0:T(8,128)(2,1)} %k_hbm.1, bf16[2,1,128,2048]{3,2,1,0:T(8,128)(2,1)} %v_hbm.1, s32[2,1,9]{2,1,0:T(1,128)} %flags_hbm.1, bf16[128,2048]{1,0:T(8,128)(2,1)} %ck_hbm.1, bf16[128,2048]{1,0:T(8,128)(2,1)} %cv_hbm.1), custom_call_target="tpu_custom_call" | custom-call | tf_op jit(solution)/shard_map/window_attention/pallas_call | solution.py:338
  94.3 2.3 %copy.8 = bf16[2,1,128,2048]{3,2,1,0:T(8,128)(2,1)} copy(bf16[2,1,128,2048]{3,2,1,0:T(8,128)(2,1)} %window_attention.1) | data formatting | bytes 2097152
